TPU v7x, 32 devices: a whole 2x2x4 slice. The times are simulated.
32 devices in a mesh: blk: 4 (over y, x), team: 4 (over z), dp: 2 (over core).
Axes of the slice: x: 2, y: 2, z: 4, core: 2. Of those that a mesh axis runs over, the one named last changes fastest.
Arguments:
- hidden: bfloat16 [1024, 28672], P(('blk', 'dp'), 'team'), may hold values from -6 to 6
- out_grad: bfloat16 [1024, 8192], P(('blk', 'dp'), 'team'), may hold values from -0.1875 to 0.1875
- act_rows: int32 [4, 64, 12], P('team'), may hold values from 0 to 55, as said below
- col_owner: int32 [64], replicated, may hold values from 0 to 3, as said below
Outputs:
- gradients: float32 [4, 4, 288, 128, 128], P('team', 'blk', 'dp')
- scores: float32 [4, 4, 288], P('team', 'blk', 'dp')
Inputs may be any that keep to these rules, and one draw needn't show every extreme that they name: For each t and c the 12 entries act_rows[t, c, :] are distinct. `col_owner`: some owner holds exactly 24 block columns and no owner holds more.
All inputs are finite; a program needn't handle non-finite values.
Results may differ from a plain program's by a relative error of at most 0.0003.
Values may be sent and summed in bfloat16 or wider, within the bound.
A program may use at most 192 MiB of HBM per device.

v0:
```python
import jax
import jax.numpy as jnp
from jax import lax
from jax.sharding import PartitionSpec as P

D = 8192
BS = 128
epsilon = 1e-06


def on_device(hidden, out_grad, act_rows, col_owner):
    owners_count = lax.axis_size("blk")
    owner_index = lax.axis_index("blk")
    column_blocks = D // BS
    capacity = min(3 * column_blocks // (2 * owners_count), 3 * column_blocks // 4)
    per_column = act_rows.shape[2]
    owners = jnp.arange(owners_count, dtype=jnp.int32)
    onehot = (col_owner[:, None] == owners[None, :]).astype(jnp.int32)
    column_rank = jnp.sum((jnp.cumsum(onehot, axis=0) - onehot) * onehot, axis=1)
    slot_ids = jnp.arange(capacity, dtype=jnp.int32)
    matches = (col_owner[None, None, :] == owners[:, None, None]) & (
        column_rank[None, None, :] == slot_ids[None, :, None]
    )
    owned_all = jnp.sum(
        matches.astype(jnp.int32) * jnp.arange(column_blocks, dtype=jnp.int32)[None, None, :],
        axis=2,
    )
    alive_all = jnp.any(matches, axis=2)
    owned_mine = lax.dynamic_index_in_dim(owned_all, owner_index, 0, keepdims=False)
    alive_mine = lax.dynamic_index_in_dim(alive_all, owner_index, 0, keepdims=False)
    block_rows = jnp.take(act_rows[0], owned_mine, axis=0).reshape(-1)
    grad_full = lax.all_gather(out_grad, "team", axis=1, tiled=True)
    grad_mask = alive_mine.astype(jnp.bfloat16)[None, :, None]
    hidden_piece = lax.all_gather(hidden, "blk", axis=0, tiled=True)
    grad_piece = lax.all_gather(grad_full, "blk", axis=0, tiled=True)
    count_rows = grad_piece.shape[0]
    picked_grad = (
        jnp.take(grad_piece.reshape(count_rows, column_blocks, BS), owned_mine, axis=1) * grad_mask
    )
    count_rows = hidden_piece.shape[0]
    hidden_blocks = hidden_piece.reshape(count_rows, -1, BS)
    picked_hidden = jnp.take(hidden_blocks, block_rows, axis=1).reshape(
        count_rows, capacity, per_column, BS
    )
    partial_value = jnp.einsum(
        "ncki,ncj->ckij", picked_hidden, picked_grad, preferred_element_type=jnp.float32
    )
    partial_value = partial_value.reshape(capacity * per_column, BS, BS)
    gradients = lax.psum_scatter(partial_value, "dp", scatter_dimension=0, tiled=True)
    scores = jnp.sqrt(jnp.mean(gradients * gradients, axis=(1, 2)) + epsilon)
    return (gradients[None, None], scores[None, None])


def solution(mesh):
    in_specs = (P(("blk", "dp"), "team"), P(("blk", "dp"), "team"), P("team", None, None), P())
    out_specs = (P("team", "blk", "dp", None, None), P("team", "blk", "dp"))
    return jax.shard_map(
        on_device, mesh=mesh, in_specs=in_specs, out_specs=out_specs, check_vma=False
    )
```

profile of v0, /device:TPU:0, one launch (start us, length us, event | category | flops | bytes accessed | tf_op | source)
XLA Modules:
  0.0 305.4 jit_solution(6852745690831261006)
XLA Ops:
  7.2 0.0 copy-start.1
  7.2 0.0 copy-start
  7.2 0.0 all-gather.6.cloned.1.call-start
  7.2 2.0 copy.20
  9.3 0.0 all-gather.6.cloned.1.call-update
  9.3 0.0 all-gather.4.cloned.1.call-start
  9.3 3.9 %copy.17 = bf16[128,7168]{0,1:T(8,128)(2,1)} copy(bf16[128,7168]{1,0:T(8,128)(2,1)} %param.4) | data formatting | bytes 3670016 | tf_op args[0]
  13.2 0.0 all-gather.4.cloned.1.call-update
  13.2 0.0 all-gather.8.cloned.1.call-start
  13.3 44.7 %all-gather.6.cloned.1.call-done = bf16[128,8192]{0,1:T(8,128)(2,1)} async-done(((bf16[128,2048]{0,1:T(8,128)(2,1)}), bf16[128,8192]{0,1:T(8,128)(2,1)}) %all-gather.6.cloned.1.call-update) | async-done | bytes 2097168 | tf_op jit(solution)/shard_map/all_gather | solution.py:32
  58.0 0.0 all-gather.8.cloned.1.call-update
  58.0 0.0 reduce-scatter.2.cloned.1.call-start
  58.1 0.0 copy-done.1
  58.1 0.1 fusion.11
  58.1 0.1 reduce_window_sum.11
  58.2 0.0 copy-done
  58.2 0.1 copy.16
  58.3 0.2 select_reduce_fusion
  58.5 0.1 fusion.10
  58.7 0.6 gather_fusion
  59.3 0.1 compare_and_fusion
  59.4 0.1 select_n.73
  59.5 0.2 and_reduce_fusion
  59.7 78.1 %all-gather.4.cloned.1.call-done = bf16[512,7168]{0,1:T(8,128)(2,1)} async-done(((bf16[128,7168]{0,1:T(8,128)(2,1)}), bf16[512,7168]{0,1:T(8,128)(2,1)}) %all-gather.4.cloned.1.call-update) | async-done | bytes 7340048 | tf_op jit(solution)/shard_map/all_gather | solution.py:34
  137.8 10.4 %copy.18 = bf16[512,56,128]{2,0,1:T(8,128)(2,1)} copy(bf16[512,56,128]{0,2,1:T(8,128)(2,1)} %bitcast.28) | data formatting | bytes 14680064 | tf_op jit(solution)/shard_map/reshape | solution.py:41
  148.3 18.8 %gather_fusion.1 = bf16[288,512,128]{2,1,0:T(8,128)(2,1)} fusion(bf16[512,56,128]{2,0,1:T(8,128)(2,1)} %copy.18, s32[1024]{0:T(1024)S(1)} %pad_clamp_fusion), kind=kCustom, calls=%fused_computation.1 | custom fusion | bytes 75498624 | tf_op jit(solution)/shard_map/jit(_take)/gather | solution.py:42
  167.1 48.8 %copy.19 = bf16[512,24,12,128]{0,3,2,1:T(8,128)(2,1)} copy(bf16[512,24,12,128]{3,0,2,1:T(8,128)(2,1)} %bitcast.24) | data formatting | bytes 75497472 | tf_op jit(solution)/shard_map/jit(_take)/gather | solution.py:42
  215.8 11.2 %all-gather.8.cloned.1.call-done = bf16[512,8192]{0,1:T(8,128)(2,1)} async-done(((bf16[128,8192]{0,1:T(8,128)(2,1)}), bf16[512,8192]{0,1:T(8,128)(2,1)}) %all-gather.8.cloned.1.call-update) | async-done | bytes 8388624 | tf_op jit(solution)/shard_map/all_gather | solution.py:35
  227.0 11.9 %copy.21 = bf16[512,64,128]{2,0,1:T(8,128)(2,1)} copy(bf16[512,64,128]{0,2,1:T(8,128)(2,1)} %bitcast.27) | data formatting | bytes 16777216 | tf_op jit(solution)/shard_map/reshape | solution.py:38
  238.9 4.5 %gather_fusion.2 = bf16[24,512,128]{2,1,0:T(8,128)(2,1)S(1)} fusion(bf16[512,64,128]{2,0,1:T(8,128)(2,1)} %copy.21, s32[1024]{0:T(1024)S(1)} %pad_clamp_fusion.1), kind=kCustom, calls=%fused_computation.2 | custom fusion | bytes 6291552 | tf_op jit(solution)/shard_map/jit(_take)/gather | solution.py:38
  243.5 23.4 %fusion = f32[24,12,128,128]{3,2,1,0:T(8,128)} fusion(bf16[512,24,12,128]{0,3,2,1:T(8,128)(2,1)} %copy.19, pred[24,12]{1,0:T(8,128)(4,1)S(1)} %get-tuple-element.2, bf16[24,512,128]{2,1,0:T(8,128)(2,1)S(1)} %gather_fusion.2, pred[24]{0:T(512)(128)(4,1)S(1)} %compare_and_fusion.1, bf16[24]{0:T(256)(128)(2,1)S(1)} %fusion.13), kind=kOutput, calls=%fused_computation.3 | convolution fusion | flops 4853858304 | bytes 59769192 | tf_op jit(solution)/shard_map/ncki,ncj->ckij/dot_general | solution.py:45
  266.8 0.0 reduce-scatter.2.cloned.1.call-update
  266.9 26.7 %reduce-scatter.2.cloned.1.call-done = f32[144,128,128]{2,1,0:T(8,128)} async-done(((f32[288,128,128]{2,1,0:T(8,128)}), f32[144,128,128]{2,1,0:T(8,128)}) %reduce-scatter.2.cloned.1.call-update) | async-done | bytes 9437200 | tf_op jit(solution)/shard_map/reduce_scatter | solution.py:49
  293.6 4.7 %multiply_reduce_fusion = f32[144]{0:T(256)S(1)} fusion(f32[144,128,128]{2,1,0:T(8,128)} %reduce-scatter.2.cloned.1.call-done), kind=kLoop, calls=%fused_computation.7 | loop fusion | flops 4718448 | bytes 9437760 | tf_op jit(solution)/shard_map/reduce_sum | solution.py:50
  298.3 0.6 add_sqrt_fusion
  (8 shorter events, 0.1 us)
Async XLA Ops:
  7.2 50.9 %copy-start.1 = (s32[64]{0:T(128)S(1)}, s32[64]{0:T(128)}, u32[]{:S(2)}) copy-start(s32[64]{0:T(128)} %param.7) | copy-start | bytes 772
  7.2 51.1 %copy-start = (s32[1,64,12]{1,0,2:T(1,128)S(1)}, s32[1,64,12]{1,0,2:T(1,128)}, u32[]{:S(2)}) copy-start(s32[1,64,12]{1,0,2:T(1,128)} %param.6) | copy-start | bytes 9220
  7.2 50.8 %all-gather.6.cloned.1.call-start = ((), (), s32[]{:S(2)}) async-start(), calls=%async_computation.2 | async-start | bytes 2621440 | tf_op jit(solution)/shard_map/all_gather | solution.py:32
  9.3 128.5 %all-gather.4.cloned.1.call-start = ((), (), s32[]{:S(2)}) async-start(), calls=%async_computation.1 | async-start | bytes 9175040 | tf_op jit(solution)/shard_map/all_gather | solution.py:34
  13.2 213.8 %all-gather.8.cloned.1.call-start = ((), (), s32[]{:S(2)}) async-start(), calls=%async_computation.3 | async-start | bytes 10485760 | tf_op jit(solution)/shard_map/all_gather | solution.py:35
  58.0 235.6 %reduce-scatter.2.cloned.1.call-start = ((), (), s32[]{:S(2)}) async-start(), calls=%async_computation.4 | async-start | bytes 28311552 | tf_op jit(solution)/shard_map/reduce_scatter | solution.py:49
Sparse Core Ops, SparseCore 0:
  9.6 48.3 all-gather.5
  60.4 77.4 all-gather.3
  139.7 87.3 all-gather.7
  267.0 26.5 reduce-scatter.1
where the time goes:
time: 307 us; the launch traced here: 305 us
  waiting for transfers between devices  161 us (52%)
  local copies, waits for them, and re-layouts  101 us (33%)
  matrix products  23.4 us (8%)
  between operations  13.9 us (5%)
  other arithmetic  6.12 us (2%)
    all_gather x1, waiting for transfers between devices, on_device(): hidden_piece = lax.all_gather(hidden, 'blk', axis=0, tiled=True)  78.1 us
    gather x2, local copies, waits for them, and re-layouts, on_device(): jnp.take(hidden_blocks, block_rows, axis=1)  67.6 us
    all_gather x1, waiting for transfers between devices, on_device(): grad_full = lax.all_gather(out_grad, 'team', axis=1, tiled=True)  44.7 us
    reduce_scatter x1, waiting for transfers between devices, on_device(): lax.psum_scatter(partial_value, 'dp', scatter_dimension=0, tiled=True)  26.7 us
    dot_general x1, matrix products, on_device(): jnp.einsum('ncki,ncj->ckij', picked_hidden, picked_grad, preferred_elemen...  23.4 us
    reshape x1, local copies, waits for them, and re-layouts, on_device(): grad_piece.reshape(count_rows, column_blocks, BS)  11.9 us
    all_gather x1, waiting for transfers between devices, on_device(): grad_piece = lax.all_gather(grad_full, 'blk', axis=0, tiled=True)  11.2 us
    reshape x1, local copies, waits for them, and re-layouts, on_device(): hidden_blocks = hidden_piece.reshape(count_rows, -1, BS)  10.4 us
  transfers between devices with their start and end apart: 4, of which 4 were waited for; matrix products, arithmetic and copies ran while one was open for 27% of the time, Pallas kernels for 0%

commit v1 on v0

--- a/solution.py
+++ b/solution.py
@@ -31,8 +31,11 @@
     block_rows = jnp.take(act_rows[0], owned_mine, axis=0).reshape(-1)
     grad_full = lax.all_gather(out_grad, "team", axis=1, tiled=True)
     grad_mask = alive_mine.astype(jnp.bfloat16)[None, :, None]
-    hidden_piece = lax.all_gather(hidden, "blk", axis=0, tiled=True)
-    grad_piece = lax.all_gather(grad_full, "blk", axis=0, tiled=True)
+    hidden_piece, grad_piece = jnp.split(
+        lax.all_gather(jnp.concatenate([hidden, grad_full], axis=1), "blk", axis=0, tiled=True),
+        [hidden.shape[1]],
+        axis=1,
+    )
     count_rows = grad_piece.shape[0]
     picked_grad = (
         jnp.take(grad_piece.reshape(count_rows, column_blocks, BS), owned_mine, axis=1) * grad_mask

time: 307 us -> 387 us (1.26)
  waiting for transfers between devices: 161 us -> 218 us
  local copies, waits for them, and re-layouts: 101 us -> 114 us
  other arithmetic: 6.12 us -> 15.4 us
    all_gather x2 -> x1, waiting for transfers between devices: 89.4 us -> 146 us  [on_device(): lax.all_gather(jnp.concatenate([hidden, grad_full], axis=1), 'blk', axis=...]
    split x0 -> x2, local copies, waits for them, and re-layouts: none -> 13.9 us  [on_device(): jnp.split(lax.all_gather(jnp.concatenate([hidden, grad_full], axis=1), 'b...]
    concatenate x0 -> x1, other arithmetic: none -> 9.28 us  [on_device(): jnp.concatenate([hidden, grad_full], axis=1)]
  transfers between devices with their start and end apart: 4 -> 3, of which waited for: 4 -> 3; matrix products, arithmetic and copies ran while one was open for 27% -> 1% of each run, Pallas kernels for 0% -> 0%
where the time goes in v1:
time: 387 us; the launch traced here: 385 us
  waiting for transfers between devices  218 us (56%)
  local copies, waits for them, and re-layouts  114 us (29%)
  matrix products  23.4 us (6%)
  other arithmetic  15.4 us (4%)
  between operations  13.9 us (4%)
    all_gather x1, waiting for transfers between devices, on_device(): lax.all_gather(jnp.concatenate([hidden, grad_full], axis=1), 'blk', axis=...  146 us
    gather x2, local copies, waits for them, and re-layouts, on_device(): jnp.take(hidden_blocks, block_rows, axis=1)  67.1 us
    all_gather x1, waiting for transfers between devices, on_device(): grad_full = lax.all_gather(out_grad, 'team', axis=1, tiled=True)  45.9 us
    reduce_scatter x1, waiting for transfers between devices, on_device(): lax.psum_scatter(partial_value, 'dp', scatter_dimension=0, tiled=True)  26.7 us
    dot_general x1, matrix products, on_device(): jnp.einsum('ncki,ncj->ckij', picked_hidden, picked_grad, preferred_elemen...  23.4 us
    split x2, local copies, waits for them, and re-layouts, on_device(): jnp.split(lax.all_gather(jnp.concatenate([hidden, grad_full], axis=1), 'b...  13.9 us
    reshape x1, local copies, waits for them, and re-layouts, on_device(): grad_piece.reshape(count_rows, column_blocks, BS)  11.9 us
    reshape x1, local copies, waits for them, and re-layouts, on_device(): hidden_blocks = hidden_piece.reshape(count_rows, -1, BS)  10.4 us
  transfers between devices with their start and end apart: 3, of which 3 were waited for; matrix products, arithmetic and copies ran while one was open for 1% of the time, Pallas kernels for 0%

profile of v1, /device:TPU:0, one launch (start us, length us, event | category | flops | bytes accessed | tf_op | source)
XLA Modules:
  0.0 385.1 jit_solution(18199390634600203848)
XLA Ops:
  7.2 0.0 all-gather.3.cloned.1.call-start
  7.2 2.0 copy.17
  9.3 0.0 all-gather.3.cloned.1.call-update
  9.3 0.0 copy-start
  9.3 0.0 copy-start.1
  9.3 0.0 all-gather.5.cloned.1.call-start
  9.3 3.3 copy.18
  12.7 45.9 %all-gather.3.cloned.1.call-done = bf16[128,8192]{0,1:T(8,128)(2,1)} async-done(((bf16[128,2048]{0,1:T(8,128)(2,1)}), bf16[128,8192]{0,1:T(8,128)(2,1)}) %all-gather.3.cloned.1.call-update) | async-done | bytes 2097168 | tf_op jit(solution)/shard_map/all_gather | solution.py:32
  58.5 9.3 %pad_maximum_fusion = bf16[128,15360]{0,1:T(8,128)(2,1)} fusion(bf16[128,8192]{0,1:T(8,128)(2,1)} %all-gather.3.cloned.1.call-done, bf16[128,7168]{0,1:T(8,128)(2,1)S(1)} %copy.18), kind=kLoop, calls=%fused_computation.8 | loop fusion | flops 7864320 | bytes 7864320 | tf_op jit(solution)/shard_map/concatenate | solution.py:35
  67.8 0.0 all-gather.5.cloned.1.call-update
  67.8 0.2 reduce-scatter.2.cloned.1.call-start
  68.1 0.0 copy-done
  68.1 0.1 copy.16
  68.2 0.0 copy-done.1
  68.2 0.1 fusion.11
  68.2 0.1 reduce_window_sum.11
  68.3 0.2 select_reduce_fusion
  68.6 0.1 fusion.10
  68.7 0.6 gather_fusion
  69.3 0.1 compare_and_fusion
  69.4 0.1 select_n.73
  69.5 0.2 and_reduce_fusion
  69.7 145.5 %all-gather.5.cloned.1.call-done = bf16[512,15360]{0,1:T(8,128)(2,1)} async-done(((bf16[128,15360]{0,1:T(8,128)(2,1)}), bf16[512,15360]{0,1:T(8,128)(2,1)}) %all-gather.5.cloned.1.call-update) | async-done | bytes 15728656 | tf_op jit(solution)/shard_map/all_gather | solution.py:35
  215.2 7.3 %split.9 = bf16[512,8192]{0,1:T(8,128)(2,1)} slice(bf16[512,15360]{0,1:T(8,128)(2,1)} %all-gather.5.cloned.1.call-done), slice={[0:512], [7168:15360]} | slice | bytes 16777216 | tf_op jit(solution)/shard_map/split | solution.py:34
  222.5 11.9 %copy.21 = bf16[512,64,128]{2,0,1:T(8,128)(2,1)} copy(bf16[512,64,128]{0,2,1:T(8,128)(2,1)} %bitcast.25) | data formatting | bytes 16777216 | tf_op jit(solution)/shard_map/reshape | solution.py:41
  234.5 4.5 %gather_fusion.2 = bf16[24,512,128]{2,1,0:T(8,128)(2,1)S(1)} fusion(bf16[512,64,128]{2,0,1:T(8,128)(2,1)} %copy.21, s32[1024]{0:T(1024)S(1)} %pad_clamp_fusion.1), kind=kCustom, calls=%fused_computation.2 | custom fusion | bytes 6291552 | tf_op jit(solution)/shard_map/jit(_take)/gather | solution.py:41
  239.0 6.6 %split.8 = bf16[512,7168]{0,1:T(8,128)(2,1)} slice(bf16[512,15360]{0,1:T(8,128)(2,1)} %all-gather.5.cloned.1.call-done), slice={[0:512], [0:7168]} | slice | bytes 14680064 | tf_op jit(solution)/shard_map/split | solution.py:34
  245.6 10.4 %copy.19 = bf16[512,56,128]{2,0,1:T(8,128)(2,1)} copy(bf16[512,56,128]{0,2,1:T(8,128)(2,1)} %bitcast.26) | data formatting | bytes 14680064 | tf_op jit(solution)/shard_map/reshape | solution.py:44
  256.0 18.4 %gather_fusion.1 = bf16[288,512,128]{2,1,0:T(8,128)(2,1)} fusion(bf16[512,56,128]{2,0,1:T(8,128)(2,1)} %copy.19, s32[1024]{0:T(1024)S(1)} %pad_clamp_fusion), kind=kCustom, calls=%fused_computation.1 | custom fusion | bytes 75498624 | tf_op jit(solution)/shard_map/jit(_take)/gather | solution.py:45
  274.4 48.7 %copy.20 = bf16[512,24,12,128]{0,3,2,1:T(8,128)(2,1)} copy(bf16[512,24,12,128]{3,0,2,1:T(8,128)(2,1)} %bitcast.24) | data formatting | bytes 75497472 | tf_op jit(solution)/shard_map/jit(_take)/gather | solution.py:45
  323.1 23.4 %fusion = f32[24,12,128,128]{3,2,1,0:T(8,128)} fusion(bf16[512,24,12,128]{0,3,2,1:T(8,128)(2,1)} %copy.20, pred[24,12]{1,0:T(8,128)(4,1)S(1)} %get-tuple-element.2, bf16[24,512,128]{2,1,0:T(8,128)(2,1)S(1)} %gather_fusion.2, pred[24]{0:T(512)(128)(4,1)S(1)} %compare_and_fusion.1, bf16[24]{0:T(256)(128)(2,1)S(1)} %fusion.13), kind=kOutput, calls=%fused_computation.3 | convolution fusion | flops 4853858304 | bytes 59769192 | tf_op jit(solution)/shard_map/ncki,ncj->ckij/dot_general | solution.py:48
  346.5 0.0 reduce-scatter.2.cloned.1.call-update
  346.5 26.7 %reduce-scatter.2.cloned.1.call-done = f32[144,128,128]{2,1,0:T(8,128)} async-done(((f32[288,128,128]{2,1,0:T(8,128)}), f32[144,128,128]{2,1,0:T(8,128)}) %reduce-scatter.2.cloned.1.call-update) | async-done | bytes 9437200 | tf_op jit(solution)/shard_map/reduce_scatter | solution.py:52
  373.3 4.7 %multiply_reduce_fusion = f32[144]{0:T(256)S(1)} fusion(f32[144,128,128]{2,1,0:T(8,128)} %reduce-scatter.2.cloned.1.call-done), kind=kLoop, calls=%fused_computation.7 | loop fusion | flops 4718448 | bytes 9437760 | tf_op jit(solution)/shard_map/reduce_sum | solution.py:53
  378.0 0.6 add_sqrt_fusion
  (8 shorter events, 0.1 us)
Async XLA Ops:
  7.2 51.4 %all-gather.3.cloned.1.call-start = ((), (), s32[]{:S(2)}) async-start(), calls=%async_computation.1 | async-start | bytes 2621440 | tf_op jit(solution)/shard_map/all_gather | solution.py:32
  9.3 58.8 %copy-start = (s32[1,64,12]{1,0,2:T(1,128)S(1)}, s32[1,64,12]{1,0,2:T(1,128)}, u32[]{:S(2)}) copy-start(s32[1,64,12]{1,0,2:T(1,128)} %param.6) | copy-start | bytes 9220
  9.3 58.9 %copy-start.1 = (s32[64]{0:T(128)S(1)}, s32[64]{0:T(128)}, u32[]{:S(2)}) copy-start(s32[64]{0:T(128)} %param.7) | copy-start | bytes 772
  9.3 205.9 %all-gather.5.cloned.1.call-start = ((), (), s32[]{:S(2)}) async-start(), calls=%async_computation.2 | async-start | bytes 19660800 | tf_op jit(solution)/shard_map/all_gather | solution.py:35
  67.8 305.4 %reduce-scatter.2.cloned.1.call-start = ((), (), s32[]{:S(2)}) async-start(), calls=%async_computation.3 | async-start | bytes 28311552 | tf_op jit(solution)/shard_map/reduce_scatter | solution.py:52
Sparse Core Ops, SparseCore 0:
  10.1 48.3 all-gather.2
  68.0 147.2 all-gather.4
  346.6 26.5 reduce-scatter.1
